TPU v7x, 32 devices: a whole 2x2x4 slice. The times are simulated.
32 devices in a mesh: dp: 16 (over z, y, x), mp: 2 (over core).
Axes of the slice: x: 2, y: 2, z: 4, core: 2. Of those that a mesh axis runs over, the one named last changes fastest.
Arguments:
- tokens: bfloat16 [8192, 2048], P('dp'), may hold values from -6 to 6
- noise_cond: float32 [128, 8192], P('dp'), may hold values from -1.5 to 1.5
- slot_bucket: int32 [16], P('dp'), may hold values from 0 to 3, as said below
- image_height: int32 [16, 8], P('dp'), may hold values from 5 to 16, as said below
- image_width: int32 [16, 8], P('dp'), may hold values from 5 to 32, as said below
- weight_query: bfloat16 [2048, 2048], P('dp', 'mp'), may hold values from -0.1875 to 0.1875
- weight_key: bfloat16 [2048, 2048], P('dp', 'mp'), may hold values from -0.1875 to 0.1875
- weight_value: bfloat16 [2048, 2048], P('dp', 'mp'), may hold values from -0.125 to 0.125
- weight_out: bfloat16 [2048, 2048], P('mp', 'dp'), may hold values from -0.5 to 0.5
- weight_in: bfloat16 [2048, 8192], P('dp', 'mp'), may hold values from -0.125 to 0.125
- weight_back: bfloat16 [8192, 2048], P('mp', 'dp'), may hold values from -0.09375 to 0.09375
- cotangent: bfloat16 [8192, 2048], P('dp'), may hold values from -6 to 6
Outputs:
- block_output: bfloat16 [8192, 2048], P('dp')
- grad_tokens: float32 [8192, 2048], P('dp')
- grad_cond: float32 [128, 8192], P('dp')
- grad_query: float32 [2048, 2048], P('dp', 'mp')
- grad_key: float32 [2048, 2048], P('dp', 'mp')
- grad_value: float32 [2048, 2048], P('dp', 'mp')
- grad_out: float32 [2048, 2048], P('mp', 'dp')
- grad_in: float32 [2048, 8192], P('dp', 'mp')
- grad_back: float32 [8192, 2048], P('mp', 'dp')
Inputs may be any that keep to these rules, and one draw needn't show every extreme that they name: `slot_bucket`: buckets 0 to 3 hold 8, 4, 2, 1 images of a slot; the first slot is of bucket 3. `image_height`: greater than half of the bucket's grid height and at most it: 8 for buckets 0 and 1, 16 for buckets 2 and 3; entries of images past the slot's count are unused. `image_width`: greater than half of the bucket's grid width and at most it: 8, 16, 16, 32 for buckets 0 to 3; entries of images past the slot's count are unused.
All inputs are finite; a program needn't handle non-finite values.
Results may differ from a plain program's by a relative error of at most 0.014.
Values may be sent and summed in bfloat16 or wider, within the bound.
No kernel may reach another device: no remote copies, remote signals or barrier semaphores. Data moves between devices by JAX's collectives and lax.ppermute only.
A program may use at most 384 MiB of HBM per device.

v0:
```python
import jax
import jax.numpy as jnp
from jax import lax
from jax.sharding import PartitionSpec as P

HD = 128
GW = 32
IMG_SLOT = 8
SLOT = 512


EPS = 1e-06
HIGH = lax.Precision.HIGHEST


def arrange(slot_bucket, image_height, image_width):
    places = jnp.arange(SLOT, dtype=jnp.int32)
    choose = (slot_bucket[:, None] == jnp.arange(4, dtype=jnp.int32)[None, :]).astype(jnp.int32)
    areas = jnp.sum(
        choose * jnp.array([SLOT // 8, SLOT // 4, SLOT // 2, SLOT], jnp.int32)[None, :], axis=1
    )
    across = jnp.sum(
        choose * jnp.array([GW // 4, GW // 2, GW // 2, GW], jnp.int32)[None, :], axis=1
    )
    image = places[None, :] // areas[:, None]
    inner = places[None, :] % areas[:, None]
    grid_row = inner // across[:, None]
    grid_col = inner % across[:, None]
    member = image[:, :, None] == jnp.arange(IMG_SLOT, dtype=jnp.int32)[None, None, :]
    tall = jnp.sum(jnp.where(member, image_height[:, None, :], 0), axis=2)
    broad = jnp.sum(jnp.where(member, image_width[:, None, :], 0), axis=2)
    real = (grid_row < tall) & (grid_col < broad)
    allowed = (image[:, :, None] == image[:, None, :]) & real[:, None, :]
    return (member.astype(jnp.float32), allowed)


def modulate(hidden_rows, member, cond_part):
    slots = member.shape[0]
    hidden = hidden_rows.reshape(slots, SLOT, -1)
    width = hidden.shape[-1]
    mods = jnp.einsum("sti,sic->stc", member, cond_part, precision=HIGH)
    factor = lax.rsqrt(jnp.mean(hidden * hidden, axis=-1, keepdims=True) + EPS)
    normed = hidden * factor * (1.0 + mods[..., :width]) + mods[..., width:]
    return normed.reshape(hidden_rows.shape)


def contract_rows(left, right):
    return lax.dot_general(
        left, right, (((0,), (0,)), ((), ())), preferred_element_type=jnp.float32
    )


def times_transposed(left, right):
    return lax.dot_general(
        left, right, (((1,), (1,)), ((), ())), preferred_element_type=jnp.float32
    )


def attend_forward(inputs):
    queries, keys_low, values, allowed = inputs
    scores = jnp.einsum(
        "qhd,khd->hqk", queries, keys_low, preferred_element_type=jnp.float32
    ) * HD ** (-0.5)
    scores = jnp.where(allowed[None], scores, -1e30)
    top = jnp.max(scores, axis=-1, keepdims=True)
    weights = jnp.where(allowed[None], jnp.exp(scores - top), 0.0)
    total = jnp.sum(weights, axis=-1, keepdims=True)
    probs = (weights / total).astype(jnp.bfloat16)
    mixed = jnp.einsum("hqk,khd->qhd", probs, values, preferred_element_type=jnp.float32)
    return (mixed.astype(jnp.bfloat16).reshape(SLOT, -1), top + jnp.log(total))


def attend_backward(inputs):
    queries, keys_low, values, allowed, logsum, grad_mixed = inputs
    scale = HD ** (-0.5)
    scores = (
        jnp.einsum("qhd,khd->hqk", queries, keys_low, preferred_element_type=jnp.float32) * scale
    )
    probs = jnp.where(allowed[None], jnp.exp(scores - logsum), 0.0)
    grad_values = jnp.einsum(
        "hqk,qhd->khd", probs.astype(jnp.bfloat16), grad_mixed, preferred_element_type=jnp.float32
    )
    grad_probs = jnp.einsum("qhd,khd->hqk", grad_mixed, values, preferred_element_type=jnp.float32)
    grad_scores = probs * (grad_probs - jnp.sum(probs * grad_probs, axis=-1, keepdims=True))
    grad_scores = grad_scores.astype(jnp.bfloat16)
    grad_queries = (
        jnp.einsum("hqk,khd->qhd", grad_scores, keys_low, preferred_element_type=jnp.float32)
        * scale
    )
    grad_keys = (
        jnp.einsum("hqk,qhd->khd", grad_scores, queries, preferred_element_type=jnp.float32) * scale
    )
    return (
        grad_queries.astype(jnp.bfloat16).reshape(SLOT, -1),
        grad_keys.astype(jnp.bfloat16).reshape(SLOT, -1),
        grad_values.astype(jnp.bfloat16).reshape(SLOT, -1),
    )


def local(
    tokens,
    noise_cond,
    slot_bucket,
    image_height,
    image_width,
    weight_query,
    weight_key,
    weight_value,
    weight_out,
    weight_in,
    weight_back,
    cotangent,
):
    member, allowed = arrange(slot_bucket, image_height, image_width)
    slots = member.shape[0]
    total_rows = tokens.shape[0]
    width = tokens.shape[1]
    cond_slots = noise_cond.reshape(slots, IMG_SLOT, 4 * width)
    first_cond = cond_slots[:, :, : 2 * width]
    second_cond = cond_slots[:, :, 2 * width :]
    query_full, key_full, value_full, out_full = (
        lax.all_gather(weight_query, "dp", axis=0, tiled=True),
        lax.all_gather(weight_key, "dp", axis=0, tiled=True),
        lax.all_gather(weight_value, "dp", axis=0, tiled=True),
        lax.all_gather(weight_out, "dp", axis=1, tiled=True),
    )
    in_full, back_full = (
        lax.all_gather(weight_in, "dp", axis=0, tiled=True),
        lax.all_gather(weight_back, "dp", axis=1, tiled=True),
    )
    local_width = query_full.shape[1]
    hidden_width = in_full.shape[1]
    hidden = tokens.astype(jnp.float32)
    first = modulate(hidden, member, first_cond).astype(jnp.bfloat16)

    def project(weight):
        made = jnp.dot(first, weight, preferred_element_type=jnp.float32).astype(jnp.bfloat16)
        return made.reshape(slots, SLOT, -1, HD)

    queries = project(query_full)
    keys_low = project(key_full)
    values = project(value_full)
    attended, logsum = lax.map(attend_forward, (queries, keys_low, values, allowed))
    attended = attended.reshape(total_rows, local_width)
    middle = hidden + lax.psum(
        jnp.dot(attended, out_full, preferred_element_type=jnp.float32), "mp"
    )
    second = modulate(middle, member, second_cond).astype(jnp.bfloat16)
    before = jnp.dot(second, in_full, preferred_element_type=jnp.float32)
    after = jax.nn.gelu(before, approximate=False).astype(jnp.bfloat16)
    result = middle + lax.psum(
        jnp.dot(after, back_full, preferred_element_type=jnp.float32).astype(jnp.bfloat16), "mp"
    ).astype(jnp.float32)
    grad_after = times_transposed(cotangent, back_full)

    def gelu_exact(pre_act):
        return jax.nn.gelu(pre_act, approximate=False)

    unused, gelu_pullback = jax.vjp(gelu_exact, before)
    grad_before = gelu_pullback(grad_after)[0].astype(jnp.bfloat16)
    grad_second = lax.psum(times_transposed(grad_before, in_full), "mp")

    def second_norm(rows_in, cond_in):
        return modulate(rows_in, member, cond_in)

    unused, second_pullback = jax.vjp(second_norm, middle, second_cond)
    grad_middle_norm, grad_second_cond = second_pullback(grad_second)
    grad_middle = cotangent.astype(jnp.float32) + grad_middle_norm
    grad_branch = grad_middle.astype(jnp.bfloat16)
    grad_attended = times_transposed(grad_branch, out_full).astype(jnp.bfloat16)
    grad_q, grad_k, grad_v = lax.map(
        attend_backward,
        (queries, keys_low, values, allowed, logsum, grad_attended.reshape(slots, SLOT, -1, HD)),
    )
    grad_q = grad_q.reshape(total_rows, local_width)
    grad_k = grad_k.reshape(total_rows, local_width)
    grad_v = grad_v.reshape(total_rows, local_width)
    grad_projected = jnp.concatenate([grad_q, grad_k, grad_v], axis=1)
    first_part = (
        times_transposed(grad_q, query_full)
        + times_transposed(grad_k, key_full)
        + times_transposed(grad_v, value_full)
    )
    grad_first = lax.psum(first_part.astype(jnp.bfloat16), "mp").astype(jnp.float32)

    def first_norm(rows_in, cond_in):
        return modulate(rows_in, member, cond_in)

    unused, first_pullback = jax.vjp(first_norm, hidden, first_cond)
    grad_hidden_norm, grad_first_cond = first_pullback(grad_first)
    grad_tokens = grad_middle + grad_hidden_norm
    grad_cond = jnp.concatenate([grad_first_cond, grad_second_cond], axis=2).reshape(
        slots * IMG_SLOT, 4 * width
    )
    every_share = lax.psum_scatter(
        jnp.concatenate(
            [
                jnp.concatenate(
                    [contract_rows(first, grad_projected), contract_rows(grad_branch, attended)],
                    axis=1,
                ),
                jnp.concatenate(
                    [contract_rows(second, grad_before), contract_rows(cotangent, after)], axis=1
                ),
            ],
            axis=1,
        ),
        "dp",
        scatter_dimension=0,
        tiled=True,
    )
    attn_share = every_share[:, : 4 * local_width]
    mlp_share = every_share[:, 4 * local_width :]
    grad_query = attn_share[:, :local_width]
    grad_key = attn_share[:, local_width : 2 * local_width]
    grad_value = attn_share[:, 2 * local_width : 3 * local_width]
    grad_out = attn_share[:, 3 * local_width :].T
    grad_in = mlp_share[:, :hidden_width]
    grad_back = mlp_share[:, hidden_width:].T
    return (
        result.astype(jnp.bfloat16),
        grad_tokens,
        grad_cond,
        grad_query,
        grad_key,
        grad_value,
        grad_out,
        grad_in,
        grad_back,
    )


def solution(mesh):
    return jax.shard_map(
        local,
        mesh=mesh,
        in_specs=(
            P("dp", None),
            P("dp", None),
            P("dp"),
            P("dp", None),
            P("dp", None),
            P("dp", "mp"),
            P("dp", "mp"),
            P("dp", "mp"),
            P("mp", "dp"),
            P("dp", "mp"),
            P("mp", "dp"),
            P("dp", None),
        ),
        out_specs=(
            P("dp", None),
            P("dp", None),
            P("dp", None),
            P("dp", "mp"),
            P("dp", "mp"),
            P("dp", "mp"),
            P("mp", "dp"),
            P("dp", "mp"),
            P("mp", "dp"),
        ),
        check_vma=False,
    )
```

profile of v0, /device:TPU:0, one launch (start us, length us, event | category | flops | bytes accessed | tf_op | source)
XLA Modules:
  0.0 3594.5 jit_solution(13039353172008248912)
XLA Ops:
  10.7 1.3 fusion.80
  15.9 0.9 and_select_fusion.3
  16.7 0.8 select_reduce_fusion.2
  17.5 1.2 and_reduce_fusion
  18.7 4.5 convolution_bitcast_fusion.2
  24.0 2.5 copy-done.5
  26.5 2.6 fusion.55
  29.2 59.9 %all-gather.9.cloned.1.call-done = bf16[2048,1024]{1,0:T(8,128)(2,1)} async-done(((bf16[128,1024]{1,0:T(8,128)(2,1)}), bf16[2048,1024]{1,0:T(8,128)(2,1)}) %all-gather.9.cloned.1.call-update) | async-done | bytes 4194320 | tf_op jit(solution)/shard_map/all_gather | solution.py:122
  89.1 6.1 convolution_convert_fusion.3
  95.2 1.7 copy.93
  96.9 69.2 %all-gather.11.cloned.1.call-done = bf16[2048,1024]{1,0:T(8,128)(2,1)} async-done(((bf16[128,1024]{1,0:T(8,128)(2,1)}), bf16[2048,1024]{1,0:T(8,128)(2,1)}) %all-gather.11.cloned.1.call-update) | async-done | bytes 4194320 | tf_op jit(solution)/shard_map/all_gather | solution.py:123
  166.1 6.1 convolution_convert_fusion.2
  172.2 2.3 copy.94
  174.5 6.1 select_reduce_fusion
  180.6 62.5 %all-gather.7.cloned.1.call-done = bf16[2048,1024]{1,0:T(8,128)(2,1)} async-done(((bf16[128,1024]{1,0:T(8,128)(2,1)}), bf16[2048,1024]{1,0:T(8,128)(2,1)}) %all-gather.7.cloned.1.call-update) | async-done | bytes 4194320 | tf_op jit(solution)/shard_map/all_gather | solution.py:124
  243.1 5.3 fusion.60
  248.4 2.0 fusion.16
  250.5 3.2 fusion.56
  253.7 79.3 %all-gather.13.cloned.1.call-done = bf16[1024,2048]{1,0:T(8,128)(2,1)} async-done(((bf16[1024,128]{1,0:T(8,128)(2,1)}), bf16[1024,2048]{1,0:T(8,128)(2,1)}) %all-gather.13.cloned.1.call-update) | async-done | bytes 4194320 | tf_op jit(solution)/shard_map/all_gather | solution.py:125
  333.0 6.6 fusion.91
  340.2 0.7 all-gather.17.cloned.1.call-update
  341.0 6.4 convolution_bitcast_fusion.1
  348.1 18.0 all-reduce.11.cloned.1.call-done
  366.0 3.0 multiply_reduce_fusion.1
  369.0 2.1 copy-done.1
  371.1 1.1 copy-done.4
  372.2 3.0 fusion.54
  375.2 185.6 %all-gather.15.cloned.1.call-done = bf16[2048,4096]{1,0:T(8,128)(2,1)} async-done(((bf16[128,4096]{1,0:T(8,128)(2,1)}), bf16[2048,4096]{1,0:T(8,128)(2,1)}) %all-gather.15.cloned.1.call-update) | async-done | bytes 16777232 | tf_op jit(solution)/shard_map/all_gather | solution.py:128
  560.9 15.0 fusion.92
  575.8 235.1 %all-gather.17.cloned.1.call-done = bf16[4096,2048]{1,0:T(8,128)(2,1)} async-done(((bf16[4096,128]{1,0:T(8,128)(2,1)}), bf16[4096,2048]{1,0:T(8,128)(2,1)}) %all-gather.17.cloned.1.call-update) | async-done | bytes 16777232 | tf_op jit(solution)/shard_map/all_gather | solution.py:129
  810.9 32.1 add_convert_fusion
  843.1 9.8 multiply_convert_fusion.1
  852.9 15.0 fusion.93
  868.0 19.2 convolution_bitcast_fusion
  887.2 15.5 fusion.96
  902.7 13.9 convolution_convert_fusion
  916.6 5.4 fusion.40
  922.5 1.3 copy-done.11
  923.7 4.8 multiply_bitcast_fusion
  928.5 2.0 copy-done.8
  930.5 2.4 convolution_convert_fusion.1
  933.5 5.3 multiply_reduce_fusion
  939.4 2.8 multiply_convert_fusion
  942.3 0.7 multiply_convert_fusion.3
  943.5 1.5 multiply_convert_fusion.2
  945.0 2.0 fusion.57
  947.5 5.7 fusion.64
  953.1 13.7 fusion.48
  966.9 2.4 fusion.94
  969.3 2.4 fusion.95
  971.8 3.9 add_convert_fusion.1
  975.7 68.3 %pad_maximum_fusion = f32[2048,12288]{1,0:T(8,128)} fusion(f32[2048,4096]{1,0:T(8,128)} %convolution_bitcast_fusion, f32[2048,4096]{1,0:T(8,128)} %fusion.96, f32[2048,1024]{1,0:T(8,128)} %fusion.64, f32[2048,3072]{1,0:T(8,128)} %fusion.48), kind=kLoop, calls=%fused_computation | loop fusion | flops 75497472 | bytes 201326592 | tf_op jit(solution)/shard_map/concatenate | solution.py:196
  1045.9 7.5 fusion.21
  1053.5 3.9 fusion.37
  1057.9 1.6 copy-done.10
  1059.5 5.1 fusion.30
  1064.7 2.8 fusion.18
  1067.5 2.1 add_convert_fusion.2
  1069.6 0.7 maximum_bitcast_fusion
  1070.3 2506.3 %all-reduce.15.cloned.1.call-done = f32[2048,12288]{1,0:T(8,128)} async-done(((f32[2048,12288]{1,0:T(8,128)}), f32[2048,12288]{1,0:T(8,128)}) %all-reduce.15.cloned.1.call-update) | async-done | bytes 100663312
  3576.6 3.2 dynamic-slice_bitcast_fusion.1
  3579.7 1.0 copy.85
  3580.7 4.7 dynamic-slice_bitcast_fusion
  3585.4 1.8 copy.86
  (120 shorter events, 9.4 us)
Async XLA Ops:
  7.2 81.9 %all-gather.9.cloned.1.call-start = ((), (), s32[]{:S(2)}) async-start(), calls=%async_computation.1 | async-start | bytes 4456448 | tf_op jit(solution)/shard_map/all_gather | solution.py:122
  7.9 158.2 %all-gather.11.cloned.1.call-start = ((), (), s32[]{:S(2)}) async-start(), calls=%async_computation.2 | async-start | bytes 4456448 | tf_op jit(solution)/shard_map/all_gather | solution.py:123
  8.7 234.4 %all-gather.7.cloned.1.call-start = ((), (), s32[]{:S(2)}) async-start(), calls=%async_computation | async-start | bytes 4456448 | tf_op jit(solution)/shard_map/all_gather | solution.py:124
  9.4 323.6 %all-gather.13.cloned.1.call-start = ((), (), s32[]{:S(2)}) async-start(), calls=%async_computation.3 | async-start | bytes 4456448 | tf_op jit(solution)/shard_map/all_gather | solution.py:125
  10.0 356.1 %all-reduce.11.cloned.1.call-start = ((), (), s32[]{:S(2)}) async-start(), calls=%async_computation.4 | async-start | bytes 8388608 | tf_op jit(solution)/shard_map/psum | solution.py:145
  16.7 324.3 %copy-start.28 = (s32[1,512]{1,0:T(1,128)}, s32[1,512]{1,0:T(1,128)S(1)}, u32[]{:S(2)}) copy-start(s32[1,512]{1,0:T(1,128)S(1)} %and_select_fusion.3) | copy-start | bytes 6148
  18.7 4.5 copy-start.6
  23.3 3.3 copy-start.5
  23.8 5.4 copy-start.36
  23.8 5.4 copy-start.32
  26.5 223.9 %copy-start.19 = (pred[512,512]{0,1:T(8,128)(4,1)}, pred[512,512]{0,1:T(8,128)(4,1)S(1)}, u32[]{:S(2)}) copy-start(pred[512,512]{0,1:T(8,128)(4,1)S(1)} %compare_and_fusion) | copy-start | bytes 786436
  96.9 77.6 %copy-start.14 = (bf16[512,1024]{0,1:T(8,128)(2,1)}, bf16[512,1024]{0,1:T(8,128)(2,1)S(1)}, u32[]{:S(2)}) copy-start(bf16[512,1024]{0,1:T(8,128)(2,1)S(1)} %copy.93) | copy-start | bytes 3145732
  243.1 5.3 copy-start
  248.4 2.1 copy-start.26
  253.7 85.9 %copy-start.17 = (bf16[8,128,512]{2,1,0:T(8,128)(2,1)}, bf16[8,128,512]{2,1,0:T(8,128)(2,1)S(1)}, u32[]{:S(2)}) copy-start(bf16[8,128,512]{2,1,0:T(8,128)(2,1)S(1)} %fusion.56) | copy-start | bytes 3145732
  339.6 1.4 copy-start.30
  339.6 221.3 %all-gather.15.cloned.1.call-start = ((), (), s32[]{:S(2)}) async-start(), calls=%async_computation.5 | async-start | bytes 17825792 | tf_op jit(solution)/shard_map/all_gather | solution.py:128
  340.2 470.7 %all-gather.17.cloned.1.call-start = ((), (), s32[]{:S(2)}) async-start(), calls=%async_computation.6 | async-start | bytes 17825792 | tf_op jit(solution)/shard_map/all_gather | solution.py:129
  340.9 575.7 %all-reduce.13.cloned.1.call-start = ((), (), s32[]{:S(2)}) async-start(), calls=%async_computation.7 | async-start | bytes 8388608 | tf_op jit(solution)/shard_map/psum | solution.py:161
  366.0 6.2 copy-start.4
  369.0 2.1 copy-start.1
  369.0 2.1 copy-start.38
  369.0 2.1 copy-start.34
  375.2 435.7 %copy-start.22 = (bf16[512,2048]{1,0:T(8,128)(2,1)S(1)}, bf16[512,2048]{1,0:T(8,128)(2,1)}, u32[]{:S(2)}) copy-start(bf16[512,2048]{1,0:T(8,128)(2,1)} %param.29) | copy-start | bytes 6291460
  867.9 185.5 %all-reduce.17.cloned.1.call-start = ((), (), s32[]{:S(2)}) async-start(), calls=%async_computation.9 | async-start | bytes 8388608 | tf_op jit(solution)/shard_map/psum | solution.py:151
  868.0 19.2 copy-start.25
  868.0 19.2 copy-start.44
  887.2 15.5 copy-start.21
  916.6 5.4 copy-start.39
  916.6 5.5 copy-start.35
  916.6 5.9 copy-start.2
  916.6 7.1 copy-start.11
  923.7 6.8 copy-start.13
  928.5 2.0 copy-start.8
  930.5 3.0 copy-start.20
  930.5 3.0 copy-start.27
  930.5 3.0 copy-start.31
  933.5 5.3 slice-start
  933.5 5.9 slice-start.1
  939.4 2.8 copy-start.16
  942.2 1.2 copy-start.15
  945.0 2.2 copy-start.9
  945.0 2.5 copy-start.18
  947.5 5.7 copy-start.23
  953.1 13.7 copy-start.40
  966.9 2.4 copy-start.41
  969.3 2.5 copy-start.42
  975.7 2600.9 %all-reduce.15.cloned.1.call-start = ((), (), s32[]{:S(2)}) async-start(), calls=%async_computation.8 | async-start | bytes 201326592
  1044.0 0.7 copy-start.43
  1044.0 1.9 copy-start.29
  1045.9 7.5 copy-start.7
  1053.4 3.9 copy-start.37
  1053.4 3.9 copy-start.12
  1057.3 2.2 copy-start.10
  1057.4 2.2 copy-start.33
  1064.7 2.8 copy-start.3
  1064.7 2.9 copy-start.24
Sparse Core Ops, SparseCore 0:
  10.7 78.3 all-gather.8
  91.9 74.1 all-gather.10
  168.9 74.1 all-gather.6
  245.7 87.3 all-gather.12
  339.7 26.2 all-reduce.10
  368.7 192.1 all-gather.14
  563.6 247.2 all-gather.16
  868.1 26.2 all-reduce.12
  975.8 27.2 all-reduce.16
  1044.2 2532.3 all-reduce.14
where the time goes:
time: 3600 us; the launch traced here: 3590 us
  waiting for transfers between devices  3220 us (89%)
  matrix products  205 us (6%)
  other arithmetic  120 us (3%)
    unnamed x11, waiting for transfers between devices  2510 us
    all_gather x1, waiting for transfers between devices, local(): lax.all_gather(weight_back, 'dp', axis=1, tiled=True)  235 us
    all_gather x1, waiting for transfers between devices, local(): lax.all_gather(weight_in, 'dp', axis=0, tiled=True)  186 us
    all_gather x1, waiting for transfers between devices, local(): lax.all_gather(weight_out, 'dp', axis=1, tiled=True)  79.3 us
  transfers between devices with their start and end apart: 10, of which 8 were waited for; matrix products, arithmetic and copies ran while one was open for 6% of the time, Pallas kernels for 0%

commit v1 on v0

v1 whole, which is shorter than its diff:
```python
import jax
import jax.numpy as jnp
from jax import lax
from jax.sharding import Mesh, PartitionSpec as P

HD = 128
GW = 32
IMG_SLOT = 8
SLOT = 512
HALF = SLOT // 2
EPS = 1e-06
HIGH = lax.Precision.HIGHEST
BF = jnp.bfloat16
F32 = jnp.float32
PAIRED = (0, 4, 1, 6, 2, 5, 3, 7)
UNPAIRED = (0, 2, 4, 6, 1, 5, 3, 7)


def arrange(slot_bucket, image_height, image_width, places):
    choose = (slot_bucket[:, None] == jnp.arange(4, dtype=jnp.int32)[None, :]).astype(jnp.int32)
    areas = jnp.sum(
        choose * jnp.array([SLOT // 8, SLOT // 4, SLOT // 2, SLOT], jnp.int32)[None, :], axis=1
    )
    across = jnp.sum(
        choose * jnp.array([GW // 4, GW // 2, GW // 2, GW], jnp.int32)[None, :], axis=1
    )
    image = places[None, :] // areas[:, None]
    inner = places[None, :] % areas[:, None]
    grid_row = inner // across[:, None]
    grid_col = inner % across[:, None]
    member = image[:, :, None] == jnp.arange(IMG_SLOT, dtype=jnp.int32)[None, None, :]
    tall = jnp.sum(jnp.where(member, image_height[:, None, :], 0), axis=2)
    broad = jnp.sum(jnp.where(member, image_width[:, None, :], 0), axis=2)
    real = (grid_row < tall) & (grid_col < broad)
    return image, real


def modulate(hidden, member, cond_part):
    width = hidden.shape[-1]
    mods = jnp.einsum("ti,ic->tc", member, cond_part, precision=HIGH)
    factor = lax.rsqrt(jnp.mean(hidden * hidden, axis=-1, keepdims=True) + EPS)
    return hidden * factor * (1.0 + mods[:, :width]) + mods[:, width:]


def contract_rows(left, right):
    return lax.dot_general(left, right, (((0,), (0,)), ((), ())), preferred_element_type=F32)


def times_transposed(left, right):
    return lax.dot_general(left, right, (((1,), (1,)), ((), ())), preferred_element_type=F32)


def times(left, right):
    return jnp.dot(left, right, preferred_element_type=F32)


def reorder(rows, order):
    blocks = rows.reshape(8, HALF, rows.shape[-1])
    return jnp.concatenate([blocks[i] for i in order], axis=0)


def heads_of(rows):
    return rows.reshape(4, SLOT, -1, HD)


def attend_forward(queries, keys_low, values, allowed):
    scores = jnp.einsum(
        "sqhd,skhd->shqk", queries, keys_low, preferred_element_type=F32
    ) * HD ** (-0.5)
    scores = jnp.where(allowed, scores, -1e30)
    top = jnp.max(scores, axis=-1, keepdims=True)
    weights = jnp.where(allowed, jnp.exp(scores - top), 0.0)
    total = jnp.sum(weights, axis=-1, keepdims=True)
    probs = (weights / total).astype(BF)
    mixed = jnp.einsum("shqk,skhd->sqhd", probs, values, preferred_element_type=F32)
    return mixed.astype(BF).reshape(4 * SLOT, -1), top + jnp.log(total)


def attend_backward(queries, keys_low, values, allowed, logsum, grad_mixed):
    scale = HD ** (-0.5)
    scores = jnp.einsum("sqhd,skhd->shqk", queries, keys_low, preferred_element_type=F32) * scale
    probs = jnp.where(allowed, jnp.exp(scores - logsum), 0.0)
    grad_values = jnp.einsum(
        "shqk,sqhd->skhd", probs.astype(BF), grad_mixed, preferred_element_type=F32
    )
    grad_probs = jnp.einsum("sqhd,skhd->shqk", grad_mixed, values, preferred_element_type=F32)
    grad_scores = probs * (grad_probs - jnp.sum(probs * grad_probs, axis=-1, keepdims=True))
    grad_scores = grad_scores.astype(BF)
    grad_queries = (
        jnp.einsum("shqk,skhd->sqhd", grad_scores, keys_low, preferred_element_type=F32) * scale
    )
    grad_keys = (
        jnp.einsum("shqk,sqhd->skhd", grad_scores, queries, preferred_element_type=F32) * scale
    )
    return tuple(
        part.astype(BF).reshape(4 * SLOT, -1) for part in (grad_queries, grad_keys, grad_values)
    )


def solution(mesh):
    outer = mesh.shape["dp"] // 4
    inner_mesh = Mesh(mesh.devices.reshape(outer, 2, 2, 2), ("o", "y", "x", "mp"))
    every = ("o", "y", "x", "mp")

    def pairs(move):
        made = []
        for o in range(outer):
            for y in range(2):
                for x in range(2):
                    for m in range(2):
                        ty, tx, tm = move(y, x, m)
                        made.append(
                            (((o * 2 + y) * 2 + x) * 2 + m, ((o * 2 + ty) * 2 + tx) * 2 + tm)
                        )
        return made

    near = pairs(lambda y, x, m: (y, 1 - x, m) if m == 0 else (1 - y, x, m))
    next_near = pairs(lambda y, x, m: (1 - y, x, m) if m == 0 else (y, 1 - x, m))
    sibling = pairs(lambda y, x, m: (y, x, 1 - m))
    offsets = {
        k: pairs(lambda y, x, m, k=k: (y ^ (k >> 1), x ^ (k & 1), m)) for k in (1, 2, 3)
    }

    def move(value, how):
        return lax.ppermute(value, every, how)

    def gather_rows(own):
        first = jnp.concatenate([own, move(own, near)], axis=0)
        second = move(first, next_near)
        return jnp.concatenate(
            [first, second, move(first, sibling), move(second, sibling)], axis=0
        )

    def scatter_rows(left, right):
        quarter = left.shape[0] // 4

        def part(i):
            return times_transposed(left[i * quarter : (i + 1) * quarter], right)

        far = part(1) + move(part(3).astype(BF), sibling).astype(F32)
        got = move(far.astype(BF), next_near)
        close = part(0) + move(part(2).astype(BF), sibling).astype(F32)
        close = close + got.astype(F32)
        return close[:HALF] + move(close[HALF:].astype(BF), near).astype(F32)

    def spread_weight(shard, blocks):
        rows = shard.shape[0]
        chip = lax.axis_index("y") * 2 + lax.axis_index("x")
        parts = shard.reshape(rows, blocks, 4, -1)
        width = parts.shape[-1]
        gathered = jnp.zeros((4, rows, blocks * width), shard.dtype)
        for k in range(4):
            there = chip ^ k
            piece = lax.dynamic_index_in_dim(parts, there, 2, keepdims=False)
            piece = piece.reshape(rows, blocks * width)
            if k:
                piece = move(piece, offsets[k])
            gathered = lax.dynamic_update_slice(gathered, piece[None], (there, 0, 0))
        gathered = gathered.reshape(4 * rows, blocks * width)
        return lax.all_gather(gathered, "o", axis=0, tiled=True)

    def collect_grad(partial, blocks):
        mine = lax.psum_scatter(partial, "o", scatter_dimension=0, tiled=True)
        chip = lax.axis_index("y") * 2 + lax.axis_index("x")
        rows = mine.shape[0] // 4
        width = mine.shape[1] // blocks
        mine = mine.reshape(4, rows, blocks, 1, width)
        result = jnp.zeros((rows, blocks, 4, width), F32)
        for k in range(4):
            there = chip ^ k
            piece = lax.dynamic_index_in_dim(mine, there, 0, keepdims=False)
            if k:
                piece = move(piece, offsets[k])
            result = lax.dynamic_update_slice(result, piece, (0, 0, there, 0))
        return result.reshape(rows, blocks, 4 * width)

    def local(
        tokens,
        noise_cond,
        slot_bucket,
        image_height,
        image_width,
        weight_query,
        weight_key,
        weight_value,
        weight_out,
        weight_in,
        weight_back,
        cotangent,
    ):
        core = lax.axis_index("mp")
        width = tokens.shape[1]
        places = (jnp.arange(SLOT, dtype=jnp.int32) + HALF * core) % SLOT
        facts = jnp.concatenate([slot_bucket[:, None], image_height, image_width], axis=1)
        facts = jnp.concatenate([facts, move(facts, near)], axis=0)
        facts = jnp.concatenate([facts, move(facts, next_near)], axis=0)
        image, real = arrange(
            facts[:, 0], facts[:, 1 : 1 + IMG_SLOT], facts[:, 1 + IMG_SLOT :], places
        )
        allowed = ((image[:, :, None] == image[:, None, :]) & real[:, None, :])[:, None]
        member = (
            image[0, :HALF, None] == jnp.arange(IMG_SLOT, dtype=jnp.int32)[None, :]
        ).astype(F32)
        first_cond = noise_cond[:, : 2 * width]
        second_cond = noise_cond[:, 2 * width :]

        qkv_full = spread_weight(
            jnp.concatenate([weight_query, weight_key, weight_value], axis=1), 3
        )
        out_full = spread_weight(weight_out.T, 1)
        in_full = spread_weight(weight_in, 1)
        back_full = spread_weight(weight_back.T, 1)

        hidden = lax.dynamic_slice(tokens, (core * HALF, 0), (HALF, width)).astype(F32)
        grad_result = lax.dynamic_slice(cotangent, (core * HALF, 0), (HALF, width))
        first = gather_rows(modulate(hidden, member, first_cond).astype(BF))
        cotangents = gather_rows(grad_result)

        qkv = reorder(times(first, qkv_full).astype(BF), PAIRED)
        part = qkv.shape[1] // 3
        queries, keys_low, values = (
            heads_of(qkv[:, i * part : (i + 1) * part]) for i in range(3)
        )
        attended, logsum = attend_forward(queries, keys_low, values, allowed)
        attended = reorder(attended, UNPAIRED)
        middle = hidden + scatter_rows(attended, out_full)
        second = gather_rows(modulate(middle, member, second_cond).astype(BF))
        before = times(second, in_full)

        def gelu_exact(pre_act):
            return jax.nn.gelu(pre_act, approximate=False)

        after, gelu_pullback = jax.vjp(gelu_exact, before)
        after = after.astype(BF)
        grad_back = collect_grad(contract_rows(cotangents, after), 1)
        grad_before = gelu_pullback(times(cotangents, back_full))[0].astype(BF)
        grad_in = collect_grad(contract_rows(second, grad_before), 1)
        grad_second = scatter_rows(grad_before, in_full)
        result = (middle + scatter_rows(after, back_full)).astype(BF)

        def norm(rows_in, cond_in):
            return modulate(rows_in, member, cond_in)

        unused, second_pullback = jax.vjp(norm, middle, second_cond)
        grad_middle_norm, grad_second_cond = second_pullback(grad_second)
        grad_middle = grad_result.astype(F32) + grad_middle_norm
        grad_branch = gather_rows(grad_middle.astype(BF))
        grad_out = collect_grad(contract_rows(grad_branch, attended), 1)
        grad_attended = reorder(times(grad_branch, out_full).astype(BF), PAIRED)
        grad_qkv = attend_backward(
            queries, keys_low, values, allowed, logsum, heads_of(grad_attended)
        )
        grad_qkv = reorder(jnp.concatenate(grad_qkv, axis=1), UNPAIRED)
        grad_qkv_weight = collect_grad(contract_rows(first, grad_qkv), 3)
        grad_first = scatter_rows(grad_qkv, qkv_full)
        unused, first_pullback = jax.vjp(norm, hidden, first_cond)
        grad_hidden_norm, grad_first_cond = first_pullback(grad_first)
        grad_tokens = grad_middle + grad_hidden_norm
        grad_cond = jnp.concatenate([grad_first_cond, grad_second_cond], axis=1)
        grad_cond = grad_cond + move(grad_cond, sibling)

        def both_halves(rows):
            other = move(rows, sibling)
            made = jnp.zeros((SLOT, width), rows.dtype)
            made = lax.dynamic_update_slice(made, rows, (core * HALF, 0))
            return lax.dynamic_update_slice(made, other, ((1 - core) * HALF, 0))

        return (
            both_halves(result),
            both_halves(grad_tokens),
            grad_cond,
            grad_qkv_weight[:, 0],
            grad_qkv_weight[:, 1],
            grad_qkv_weight[:, 2],
            grad_out[:, 0].T,
            grad_in[:, 0],
            grad_back[:, 0].T,
        )

    dp = ("o", "y", "x")
    return jax.shard_map(
        local,
        mesh=inner_mesh,
        in_specs=(
            P(dp, None),
            P(dp, None),
            P(dp),
            P(dp, None),
            P(dp, None),
            P(dp, "mp"),
            P(dp, "mp"),
            P(dp, "mp"),
            P("mp", dp),
            P(dp, "mp"),
            P("mp", dp),
            P(dp, None),
        ),
        out_specs=(
            P(dp, None),
            P(dp, None),
            P(dp, None),
            P(dp, "mp"),
            P(dp, "mp"),
            P(dp, "mp"),
            P("mp", dp),
            P(dp, "mp"),
            P("mp", dp),
        ),
        check_vma=False,
    )
```

time: 3600 us -> 1040 us (0.29)
  waiting for transfers between devices: 3220 us -> 501 us
  local copies, waits for them, and re-layouts: 29 us -> 197 us
  starting transfers between devices: 0.39 us -> 70.7 us
  other arithmetic: 120 us -> 55.2 us
    unnamed x11 -> x8, waiting for transfers between devices: 2510 us -> 0.13 us
    all_gather x6 -> x4, waiting for transfers between devices: 692 us -> 37 us  [spread_weight(): return lax.all_gather(gathered, 'o', axis=0, tiled=True)]
    ppermute x0 -> x61, waiting for transfers between devices: none -> 239 us  [move(): return lax.ppermute(value, every, how)]
    reduce_scatter x0 -> x4, waiting for transfers between devices: none -> 225 us  [collect_grad(): mine = lax.psum_scatter(partial, 'o', scatter_dimension=0, tiled=True)]
    ppermute x0 -> x61, starting transfers between devices: none -> 70.2 us  [move(): return lax.ppermute(value, every, how)]
    concatenate x1 -> x9, other arithmetic: 68.3 us -> 7.73 us  [the longest x4 6.05 us: gather_rows(): first = jnp.concatenate([own, move(own, near)], axis=0)]
    dynamic_update_slice x0 -> x34, local copies, waits for them, and re-layouts: none -> 60.6 us  [the longest x16 46.2 us: collect_grad(): result = lax.dynamic_update_slice(result, piece, (0, 0, there, 0))]
    unnamed x97 -> x214, local copies, waits for them, and re-layouts: 16.7 us -> 57.5 us
  transfers between devices with their start and end apart: 10 -> 69, of which waited for: 8 -> 25; matrix products, arithmetic and copies ran while one was open for 6% -> 36% of each run, Pallas kernels for 0% -> 0%
where the time goes in v1:
time: 1040 us
  waiting for transfers between devices  501 us (48%)
  local copies, waits for them, and re-layouts  197 us (19%)
  matrix products  196 us (19%)
  starting transfers between devices  70.7 us (7%)
  other arithmetic  55.2 us (5%)
  between operations  17.1 us (2%)
    ppermute x61, waiting for transfers between devices, move(): return lax.ppermute(value, every, how)  239 us
    reduce_scatter x4, waiting for transfers between devices, collect_grad(): mine = lax.psum_scatter(partial, 'o', scatter_dimension=0, tiled=True)  225 us
    ppermute x61, starting transfers between devices, move(): return lax.ppermute(value, every, how)  70.2 us
    dot_general x4, matrix products, times(): return jnp.dot(left, right, preferred_element_type=F32)  63 us
    unnamed x214, local copies, waits for them, and re-layouts  57.5 us
    dot_general x16, matrix products, times_transposed(): lax.dot_general(left, right, (((1,), (1,)), ((), ())), preferred_element_...  56.4 us
    dynamic_update_slice x16, local copies, waits for them, and re-layouts, collect_grad(): result = lax.dynamic_update_slice(result, piece, (0, 0, there, 0))  46.2 us
    dot_general x4, matrix products, contract_rows(): lax.dot_general(left, right, (((0,), (0,)), ((), ())), preferred_element_...  45.7 us
  transfers between devices with their start and end apart: 69, of which 25 were waited for; matrix products, arithmetic and copies ran while one was open for 36% of the time, Pallas kernels for 0%

profile of v1, /device:TPU:0, one launch (start us, length us, event | category | flops | bytes accessed | tf_op | source)
XLA Modules:
  0.0 1036.5 jit_solution(10898821490958238784)
XLA Ops:
  22.3 5.6 collective-permute-done.1
  40.4 9.0 collective-permute-done.2
  55.9 22.7 %collective-permute-done.3 = bf16[512,2048]{1,0:T(8,128)(2,1)} collective-permute-done((bf16[512,2048]{1,0:T(8,128)(2,1)}, bf16[512,2048]{1,0:T(8,128)(2,1)}, u32[]{:S(2)}, u32[]{:S(2)}) %collective-permute-start.3) | collective-permute-done | bytes 2097184 | tf_op jit(solution)/shard_map/ppermute | solution.py:125
  86.5 3.2 constant_dynamic-update-slice_fusion.1
  89.7 3.2 constant_dynamic-update-slice_fusion
  92.9 11.5 %all-gather.5.cloned.1.call-done = bf16[2048,768]{1,0:T(8,128)(2,1)} async-done(((bf16[512,768]{1,0:T(8,128)(2,1)}), bf16[2048,768]{1,0:T(8,128)(2,1)}) %all-gather.5.cloned.1.call-update) | async-done | bytes 3145744 | tf_op jit(solution)/shard_map/all_gather | solution.py:160
  104.4 10.0 convolution_convert_fusion
  130.8 3.3 fusion.43
  136.7 3.3 convolution_convert_fusion.5
  150.4 3.7 add_convert_fusion.4
  160.3 20.7 %collective-permute-done.14 = bf16[512,2048]{1,0:T(8,128)(2,1)} collective-permute-done((bf16[512,2048]{1,0:T(8,128)(2,1)}, bf16[512,2048]{1,0:T(8,128)(2,1)}, u32[]{:S(2)}, u32[]{:S(2)}) %collective-permute-start.14) | collective-permute-done | bytes 2097184 | tf_op jit(solution)/shard_map/ppermute | solution.py:125
  181.0 3.5 convert_add_fusion.3
  189.9 9.6 collective-permute-done.15
  203.4 7.4 collective-permute-done.31
  227.3 8.8 collective-permute-done.23
  241.9 9.2 collective-permute-done.24
  254.6 7.1 collective-permute-start.33
  262.2 14.2 %collective-permute-done.17 = bf16[512,2048]{1,0:T(8,128)(2,1)} collective-permute-done((bf16[512,2048]{1,0:T(8,128)(2,1)}, bf16[512,2048]{1,0:T(8,128)(2,1)}, u32[]{:S(2)}, u32[]{:S(2)}) %collective-permute-start.17) | collective-permute-done | bytes 2097184 | tf_op jit(solution)/shard_map/ppermute | solution.py:125
  276.4 6.6 collective-permute-start.19
  285.3 3.2 constant_dynamic-update-slice_fusion.12
  293.8 3.2 constant_dynamic-update-slice_fusion.7
  299.9 14.9 %fusion.132 = f32[2048,1024]{1,0:T(8,128)} fusion(bf16[2048,2048]{1,0:T(8,128)(2,1)} %constant_dynamic-update-slice_fusion.5, bf16[2048,1024]{1,0:T(8,128)(2,1)} %all-gather.9.cloned.1.call-done), kind=kOutput, calls=%fused_computation.344 | convolution fusion | flops 8589934592 | bytes 20971520 | tf_op jit(solution)/shard_map/dot_general | solution.py:54
  314.9 25.5 %all-gather.11.cloned.1.call-done = bf16[2048,1024]{1,0:T(8,128)(2,1)} async-done(((bf16[512,1024]{1,0:T(8,128)(2,1)}), bf16[2048,1024]{1,0:T(8,128)(2,1)}) %all-gather.11.cloned.1.call-update) | async-done | bytes 4194320 | tf_op jit(solution)/shard_map/all_gather | solution.py:160
  340.3 32.3 %add_convert_fusion = (bf16[2048,1024]{1,0:T(8,128)(2,1)S(1)}, f32[2048,1024]{1,0:T(8,128)}) fusion(f32[2048,1024]{1,0:T(8,128)} %fusion.132, bf16[2048,2048]{1,0:T(8,128)(2,1)} %constant_dynamic-update-slice_fusion.10, bf16[2048,1024]{1,0:T(8,128)(2,1)} %all-gather.11.cloned.1.call-done), kind=kOutput, calls=%fused_computation.5 | convolution fusion | flops 8740929536 | bytes 33554432 | tf_op jit(solution)/shard_map/dot_general | solution.py:54
  372.7 3.7 convolution_convert_fusion.1
  376.4 10.2 multiply_convert_fusion.1
  386.6 5.0 convolution_convert_fusion.3
  392.3 3.7 convolution_convert_fusion.2
  396.0 5.5 add_convert_fusion.2
  402.9 4.1 convolution_convert_fusion.4
  407.3 3.7 add_convert_fusion.3
  412.5 3.6 fusion.49
  416.1 11.6 %collective-permute-done.37 = bf16[512,2048]{1,0:T(8,128)(2,1)S(1)} collective-permute-done((bf16[512,2048]{1,0:T(8,128)(2,1)}, bf16[512,2048]{1,0:T(8,128)(2,1)S(1)}, u32[]{:S(2)}, u32[]{:S(2)}) %collective-permute-start.37) | collective-permute-done | bytes 2097184 | tf_op jit(solution)/shard_map/ppermute | solution.py:125
  432.9 28.5 %collective-permute-done.28 = bf16[512,2048]{1,0:T(8,128)(2,1)S(1)} collective-permute-done((bf16[512,2048]{1,0:T(8,128)(2,1)}, bf16[512,2048]{1,0:T(8,128)(2,1)S(1)}, u32[]{:S(2)}, u32[]{:S(2)}) %collective-permute-start.28) | collective-permute-done | bytes 2097184 | tf_op jit(solution)/shard_map/ppermute | solution.py:125
  466.7 10.7 %collective-permute-done.29 = bf16[256,2048]{1,0:T(8,128)(2,1)S(1)} collective-permute-done((bf16[256,2048]{1,0:T(8,128)(2,1)S(1)}, bf16[256,2048]{1,0:T(8,128)(2,1)S(1)}, u32[]{:S(2)}, u32[]{:S(2)}) %collective-permute-start.29) | collective-permute-done | bytes 1048608 | tf_op jit(solution)/shard_map/ppermute | solution.py:125
  482.2 13.3 %collective-permute-done.39 = bf16[256,2048]{1,0:T(8,128)(2,1)S(1)} collective-permute-done((bf16[256,2048]{1,0:T(8,128)(2,1)S(1)}, bf16[256,2048]{1,0:T(8,128)(2,1)S(1)}, u32[]{:S(2)}, u32[]{:S(2)}) %collective-permute-start.39) | collective-permute-done | bytes 1048608 | tf_op jit(solution)/shard_map/ppermute | solution.py:125
  497.4 24.4 %collective-permute-done.40 = bf16[512,2048]{1,0:T(8,128)(2,1)S(1)} collective-permute-done((bf16[512,2048]{1,0:T(8,128)(2,1)S(1)}, bf16[512,2048]{1,0:T(8,128)(2,1)S(1)}, u32[]{:S(2)}, u32[]{:S(2)}) %collective-permute-start.40) | collective-permute-done | bytes 2097184 | tf_op jit(solution)/shard_map/ppermute | solution.py:125
  527.8 7.3 fusion.134
  535.1 14.7 %fusion.135 = f32[2048,1024]{1,0:T(8,128)} fusion(bf16[2048,2048]{1,0:T(8,128)(2,1)} %constant_dynamic-update-slice_fusion.5, bf16[2048,1024]{1,0:T(8,128)(2,1)} %copy-done.75), kind=kOutput, calls=%fused_computation.347 | convolution fusion | flops 8589934592 | bytes 20971520 | tf_op jit(solution)/shard_map/dot_general | solution.py:46
  549.9 14.7 %fusion.136 = f32[2048,1024]{1,0:T(8,128)} fusion(bf16[2048,2048]{1,0:T(8,128)(2,1)} %constant_dynamic-update-slice_fusion.10, bf16[2048,1024]{1,0:T(8,128)(2,1)} %multiply_convert_fusion.1), kind=kOutput, calls=%fused_computation.348 | convolution fusion | flops 8589934592 | bytes 20971520 | tf_op jit(solution)/shard_map/dot_general | solution.py:46
  565.8 5.7 convolution_convert_fusion.9
  573.2 6.8 fusion.40
  580.0 3.7 copy.199
  583.7 6.1 multiply_reduce_fusion
  589.8 4.9 multiply_convert_fusion
  599.0 4.1 fusion.44
  609.6 9.1 fusion.133
  618.7 3.9 convolution_convert_fusion.7
  623.1 3.2 convolution_convert_fusion.8
  631.6 3.7 fusion.59
  635.4 21.0 %collective-permute-done.45 = bf16[512,2048]{1,0:T(8,128)(2,1)} collective-permute-done((bf16[512,2048]{1,0:T(8,128)(2,1)}, bf16[512,2048]{1,0:T(8,128)(2,1)}, u32[]{:S(2)}, u32[]{:S(2)}) %collective-permute-start.45) | collective-permute-done | bytes 2097184 | tf_op jit(solution)/shard_map/ppermute | solution.py:125
  673.9 7.9 collective-permute-done.52
  694.1 29.4 %reduce-scatter.9.cloned.1.call-done = f32[512,1024]{1,0:T(8,128)} async-done(((f32[2048,1024]{1,0:T(8,128)}), f32[512,1024]{1,0:T(8,128)}) %reduce-scatter.9.cloned.1.call-update) | async-done | bytes 2097168 | tf_op jit(solution)/shard_map/reduce_scatter | solution.py:163
  734.4 136.8 %reduce-scatter.11.cloned.1.call-done = f32[512,1024]{1,0:T(8,128)} async-done(((f32[2048,1024]{1,0:T(8,128)}), f32[512,1024]{1,0:T(8,128)}) %reduce-scatter.11.cloned.1.call-update) | async-done | bytes 2097168 | tf_op jit(solution)/shard_map/reduce_scatter | solution.py:163
  882.9 4.1 dynamic_update_slice.136
  890.9 4.1 dynamic_update_slice.137
  895.6 4.1 dynamic_update_slice.138
  899.7 11.3 %collective-permute-done.57 = f32[128,1,1,1024]{3,0,2,1:T(8,128)} collective-permute-done((f32[128,1,1,1024]{3,0,2,1:T(8,128)}, f32[128,1,1,1024]{3,0,2,1:T(8,128)}, u32[]{:S(2)}, u32[]{:S(2)}) %collective-permute-start.57) | collective-permute-done | bytes 524320 | tf_op jit(solution)/shard_map/ppermute | solution.py:125
  912.6 4.1 dynamic_update_slice.139
  925.9 59.0 %reduce-scatter.5.cloned.1.call-done = f32[512,768]{1,0:T(8,128)} async-done(((f32[2048,768]{1,0:T(8,128)}), f32[512,768]{1,0:T(8,128)}) %reduce-scatter.5.cloned.1.call-update) | async-done | bytes 1572880 | tf_op jit(solution)/shard_map/reduce_scatter | solution.py:163
  1001.3 5.6 dynamic_update_slice.128
  1008.4 5.9 dynamic_update_slice.129
  1015.7 5.6 dynamic_update_slice.130
  1021.8 5.6 dynamic_update_slice.131
  (484 shorter events, 257.0 us)
Async XLA Ops:
  7.2 97.2 %all-gather.5.cloned.1.call-start = ((), (), s32[]{:S(2)}) async-start(), calls=%async_computation.4 | async-start | bytes 3932160 | tf_op jit(solution)/shard_map/all_gather | solution.py:160
  8.8 11.8 %collective-permute-start = (s32[1,17]{1,0:T(1,128)S(1)}, s32[1,17]{1,0:T(1,128)S(1)}, u32[]{:S(2)}, u32[]{:S(2)}) collective-permute-start(s32[1,17]{1,0:T(1,128)S(1)} %pad_add_fusion.2), channel_id=1, source_target_pairs={{0,2},{1,5},{2,0},{3,7},{4,6},{5,1},{6,4},{7,3},{8,10},{9,13},{10,... | collective-permute-start | bytes 212 | tf_op jit(solution)/shard_map/ppermute | solution.py:125
  16.0 19.1 %collective-permute-start.6 = (bf16[128,768]{0,1:T(8,128)(2,1)}, bf16[128,768]{0,1:T(8,128)(2,1)}, u32[]{:S(2)}, u32[]{:S(2)}) collective-permute-start(bf16[128,768]{0,1:T(8,128)(2,1)} %bitcast.4), channel_id=1, source_target_pairs={{0,2},{1,3},{2,0},{3,1},{4,6},{5,7},{6,4},{7,5},{8,10},{9,11},{10,... | collective-permute-start | bytes 589832 | tf_op jit(solution)/shard_map/ppermute | solution.py:125
  16.0 20.1 %collective-permute-start.7 = (bf16[128,768]{0,1:T(8,128)(2,1)S(1)}, bf16[128,768]{0,1:T(8,128)(2,1)}, u32[]{:S(2)}, u32[]{:S(2)}) collective-permute-start(bf16[128,768]{0,1:T(8,128)(2,1)S(1)} %bitcast.243), channel_id=1, source_target_pairs={{0,4},{1,5},{2,6},{3,7},{4,0},{5,1},{6,2},{7,3},{8,12},{9,13},{10,... | collective-permute-start | bytes 589832 | tf_op jit(solution)/shard_map/ppermute | solution.py:125
  18.1 19.2 %collective-permute-start.8 = (bf16[128,768]{0,1:T(8,128)(2,1)S(1)}, bf16[128,768]{0,1:T(8,128)(2,1)}, u32[]{:S(2)}, u32[]{:S(2)}) collective-permute-start(bf16[128,768]{0,1:T(8,128)(2,1)S(1)} %bitcast.242), channel_id=1, source_target_pairs={{0,6},{1,7},{2,4},{3,5},{4,2},{5,3},{6,0},{7,1},{8,14},{9,15},{10,... | collective-permute-start | bytes 589832 | tf_op jit(solution)/shard_map/ppermute | solution.py:125
  34.6 14.8 %collective-permute-start.2 = (bf16[256,2048]{1,0:T(8,128)(2,1)S(1)}, bf16[256,2048]{1,0:T(8,128)(2,1)S(1)}, u32[]{:S(2)}, u32[]{:S(2)}) collective-permute-start(bf16[256,2048]{1,0:T(8,128)(2,1)S(1)} %get-tuple-element.33), channel_id=1, source_target_pairs={{0,2},{1,5},{2,0},{3,7},{4,6},{5,1},{6,4},{7,3},{8,10},{9,13},{10,... | collective-permute-start | bytes 3145736 | tf_op jit(solution)/shard_map/ppermute | solution.py:125
  40.4 96.1 %all-gather.7.cloned.1.call-start = ((), (), s32[]{:S(2)}) async-start(), calls=%async_computation.5 | async-start | bytes 1310720 | tf_op jit(solution)/shard_map/all_gather | solution.py:160
  50.9 27.8 %collective-permute-start.3 = (bf16[512,2048]{1,0:T(8,128)(2,1)}, bf16[512,2048]{1,0:T(8,128)(2,1)}, u32[]{:S(2)}, u32[]{:S(2)}) collective-permute-start(bf16[512,2048]{1,0:T(8,128)(2,1)} %pad_maximum_fusion), channel_id=1, source_target_pairs={{0,4},{1,3},{2,6},{3,1},{4,0},{5,7},{6,2},{7,5},{8,12},{9,11},{10,... | collective-permute-start | bytes 6291464 | tf_op jit(solution)/shard_map/ppermute | solution.py:125
  51.0 30.0 %collective-permute-start.9 = (bf16[128,256]{1,0:T(8,128)(2,1)S(1)}, bf16[128,256]{1,0:T(8,128)(2,1)S(1)}, u32[]{:S(2)}, u32[]{:S(2)}) collective-permute-start(bf16[128,256]{1,0:T(8,128)(2,1)S(1)} %bitcast.250), channel_id=1, source_target_pairs={{0,2},{1,3},{2,0},{3,1},{4,6},{5,7},{6,4},{7,5},{8,10},{9,11},{10,... | collective-permute-start | bytes 196616 | tf_op jit(solution)/shard_map/ppermute | solution.py:125
  51.7 29.4 %collective-permute-start.10 = (bf16[128,256]{1,0:T(8,128)(2,1)S(1)}, bf16[128,256]{1,0:T(8,128)(2,1)S(1)}, u32[]{:S(2)}, u32[]{:S(2)}) collective-permute-start(bf16[128,256]{1,0:T(8,128)(2,1)S(1)} %bitcast.249), channel_id=1, source_target_pairs={{0,4},{1,5},{2,6},{3,7},{4,0},{5,1},{6,2},{7,3},{8,12},{9,13},{10,... | collective-permute-start | bytes 196616 | tf_op jit(solution)/shard_map/ppermute | solution.py:125
  53.9 27.3 %collective-permute-start.11 = (bf16[128,256]{1,0:T(8,128)(2,1)S(1)}, bf16[128,256]{1,0:T(8,128)(2,1)S(1)}, u32[]{:S(2)}, u32[]{:S(2)}) collective-permute-start(bf16[128,256]{1,0:T(8,128)(2,1)S(1)} %bitcast.248), channel_id=1, source_target_pairs={{0,6},{1,7},{2,4},{3,5},{4,2},{5,3},{6,0},{7,1},{8,14},{9,15},{10,... | collective-permute-start | bytes 196616 | tf_op jit(solution)/shard_map/ppermute | solution.py:125
  55.1 31.3 %collective-permute-start.4 = (bf16[512,2048]{1,0:T(8,128)(2,1)}, bf16[512,2048]{1,0:T(8,128)(2,1)}, u32[]{:S(2)}, u32[]{:S(2)}) collective-permute-start(bf16[512,2048]{1,0:T(8,128)(2,1)} %pad_maximum_fusion), channel_id=1, source_target_pairs={{0,1},{1,0},{2,3},{3,2},{4,5},{5,4},{6,7},{7,6},{8,9},{9,8},{10,11... | collective-permute-start | bytes 6291464 | tf_op jit(solution)/shard_map/ppermute | solution.py:125
  78.6 11.0 %collective-permute-start.5 = (bf16[512,2048]{1,0:T(8,128)(2,1)}, bf16[512,2048]{1,0:T(8,128)(2,1)}, u32[]{:S(2)}, u32[]{:S(2)}) collective-permute-start(bf16[512,2048]{1,0:T(8,128)(2,1)} %collective-permute-done.3), channel_id=1, source_target_pairs={{0,1},{1,0},{2,3},{3,2},{4,5},{5,4},{6,7},{7,6},{8,9},{9,8},{10,11... | collective-permute-start | bytes 6291464 | tf_op jit(solution)/shard_map/ppermute | solution.py:125
  82.0 218.0 %all-gather.9.cloned.1.call-start = ((), (), s32[]{:S(2)}) async-start(), calls=%async_computation.6 | async-start | bytes 5242880 | tf_op jit(solution)/shard_map/all_gather | solution.py:160
  140.0 10.4 %collective-permute-start.13 = (bf16[512,2048]{1,0:T(8,128)(2,1)}, bf16[512,2048]{1,0:T(8,128)(2,1)}, u32[]{:S(2)}, u32[]{:S(2)}) collective-permute-start(bf16[512,2048]{1,0:T(8,128)(2,1)} %convolution_convert_fusion.5), channel_id=1, source_target_pairs={{0,1},{1,0},{2,3},{3,2},{4,5},{5,4},{6,7},{7,6},{8,9},{9,8},{10,11... | collective-permute-start | bytes 6291464 | tf_op jit(solution)/shard_map/ppermute | solution.py:125
  141.8 13.8 %collective-permute-start.20 = (bf16[128,1024]{1,0:T(8,128)(2,1)}, bf16[128,1024]{1,0:T(8,128)(2,1)}, u32[]{:S(2)}, u32[]{:S(2)}) collective-permute-start(bf16[128,1024]{1,0:T(8,128)(2,1)} %bitcast.33), channel_id=1, source_target_pairs={{0,2},{1,3},{2,0},{3,1},{4,6},{5,7},{6,4},{7,5},{8,10},{9,11},{10,... | collective-permute-start | bytes 786440 | tf_op jit(solution)/shard_map/ppermute | solution.py:125
  144.2 14.3 %collective-permute-start.21 = (bf16[128,1024]{1,0:T(8,128)(2,1)}, bf16[128,1024]{1,0:T(8,128)(2,1)S(1)}, u32[]{:S(2)}, u32[]{:S(2)}) collective-permute-start(bf16[128,1024]{1,0:T(8,128)(2,1)} %bitcast.35), channel_id=1, source_target_pairs={{0,4},{1,5},{2,6},{3,7},{4,0},{5,1},{6,2},{7,3},{8,12},{9,13},{10,... | collective-permute-start | bytes 786440 | tf_op jit(solution)/shard_map/ppermute | solution.py:125
  146.5 12.0 %collective-permute-start.22 = (bf16[128,1024]{1,0:T(8,128)(2,1)}, bf16[128,1024]{1,0:T(8,128)(2,1)S(1)}, u32[]{:S(2)}, u32[]{:S(2)}) collective-permute-start(bf16[128,1024]{1,0:T(8,128)(2,1)} %bitcast.37), channel_id=1, source_target_pairs={{0,6},{1,7},{2,4},{3,5},{4,2},{5,3},{6,0},{7,1},{8,14},{9,15},{10,... | collective-permute-start | bytes 786440 | tf_op jit(solution)/shard_map/ppermute | solution.py:125
  154.1 26.9 %collective-permute-start.14 = (bf16[512,2048]{1,0:T(8,128)(2,1)}, bf16[512,2048]{1,0:T(8,128)(2,1)}, u32[]{:S(2)}, u32[]{:S(2)}) collective-permute-start(bf16[512,2048]{1,0:T(8,128)(2,1)} %add_convert_fusion.4), channel_id=1, source_target_pairs={{0,4},{1,3},{2,6},{3,1},{4,0},{5,7},{6,2},{7,5},{8,12},{9,11},{10,... | collective-permute-start | bytes 6291464 | tf_op jit(solution)/shard_map/ppermute | solution.py:125
  159.5 180.9 %all-gather.11.cloned.1.call-start = ((), (), s32[]{:S(2)}) async-start(), calls=%async_computation.7 | async-start | bytes 5242880 | tf_op jit(solution)/shard_map/all_gather | solution.py:160
  184.6 14.9 %collective-permute-start.15 = (bf16[256,2048]{1,0:T(8,128)(2,1)S(1)}, bf16[256,2048]{1,0:T(8,128)(2,1)S(1)}, u32[]{:S(2)}, u32[]{:S(2)}) collective-permute-start(bf16[256,2048]{1,0:T(8,128)(2,1)S(1)} %slice.472), channel_id=1, source_target_pairs={{0,2},{1,5},{2,0},{3,7},{4,6},{5,1},{6,4},{7,3},{8,10},{9,13},{10,... | collective-permute-start | bytes 3145736 | tf_op jit(solution)/shard_map/ppermute | solution.py:125
  186.9 23.8 %collective-permute-start.31 = (bf16[256,2048]{1,0:T(8,128)(2,1)S(1)}, bf16[256,2048]{1,0:T(8,128)(2,1)S(1)}, u32[]{:S(2)}, u32[]{:S(2)}) collective-permute-start(bf16[256,2048]{1,0:T(8,128)(2,1)S(1)} %get-tuple-element.25), channel_id=1, source_target_pairs={{0,2},{1,5},{2,0},{3,7},{4,6},{5,1},{6,4},{7,3},{8,10},{9,13},{10,... | collective-permute-start | bytes 3145736 | tf_op jit(solution)/shard_map/ppermute | solution.py:125
  202.4 35.3 %collective-permute-start.16 = (bf16[256,2048]{1,0:T(8,128)(2,1)S(1)}, bf16[256,2048]{1,0:T(8,128)(2,1)}, u32[]{:S(2)}, u32[]{:S(2)}) collective-permute-start(bf16[256,2048]{1,0:T(8,128)(2,1)S(1)} %get-tuple-element.29), channel_id=1, source_target_pairs={{0,2},{1,5},{2,0},{3,7},{4,6},{5,1},{6,4},{7,3},{8,10},{9,13},{10,... | collective-permute-start | bytes 3145736 | tf_op jit(solution)/shard_map/ppermute | solution.py:125
  212.4 49.3 %collective-permute-start.32 = (bf16[512,2048]{1,0:T(8,128)(2,1)}, bf16[512,2048]{1,0:T(8,128)(2,1)}, u32[]{:S(2)}, u32[]{:S(2)}) collective-permute-start(bf16[512,2048]{1,0:T(8,128)(2,1)} %pad_maximum_fusion.2), channel_id=1, source_target_pairs={{0,4},{1,3},{2,6},{3,1},{4,0},{5,7},{6,2},{7,5},{8,12},{9,11},{10,... | collective-permute-start | bytes 6291464 | tf_op jit(solution)/shard_map/ppermute | solution.py:125
  216.6 19.5 %collective-permute-start.23 = (bf16[128,1024]{1,0:T(8,128)(2,1)}, bf16[128,1024]{1,0:T(8,128)(2,1)}, u32[]{:S(2)}, u32[]{:S(2)}) collective-permute-start(bf16[128,1024]{1,0:T(8,128)(2,1)} %bitcast.238), channel_id=1, source_target_pairs={{0,2},{1,3},{2,0},{3,1},{4,6},{5,7},{6,4},{7,5},{8,10},{9,11},{10,... | collective-permute-start | bytes 786440 | tf_op jit(solution)/shard_map/ppermute | solution.py:125
  219.3 31.8 %collective-permute-start.24 = (bf16[128,1024]{1,0:T(8,128)(2,1)}, bf16[128,1024]{1,0:T(8,128)(2,1)}, u32[]{:S(2)}, u32[]{:S(2)}) collective-permute-start(bf16[128,1024]{1,0:T(8,128)(2,1)} %bitcast.237), channel_id=1, source_target_pairs={{0,4},{1,5},{2,6},{3,7},{4,0},{5,1},{6,2},{7,3},{8,12},{9,13},{10,... | collective-permute-start | bytes 786440 | tf_op jit(solution)/shard_map/ppermute | solution.py:125
  221.7 31.2 %collective-permute-start.25 = (bf16[128,1024]{1,0:T(8,128)(2,1)}, bf16[128,1024]{1,0:T(8,128)(2,1)}, u32[]{:S(2)}, u32[]{:S(2)}) collective-permute-start(bf16[128,1024]{1,0:T(8,128)(2,1)} %bitcast.236), channel_id=1, source_target_pairs={{0,6},{1,7},{2,4},{3,5},{4,2},{5,3},{6,0},{7,1},{8,14},{9,15},{10,... | collective-permute-start | bytes 786440 | tf_op jit(solution)/shard_map/ppermute | solution.py:125
  240.5 35.9 %collective-permute-start.17 = (bf16[512,2048]{1,0:T(8,128)(2,1)}, bf16[512,2048]{1,0:T(8,128)(2,1)}, u32[]{:S(2)}, u32[]{:S(2)}) collective-permute-start(bf16[512,2048]{1,0:T(8,128)(2,1)} %pad_maximum_fusion.1), channel_id=1, source_target_pairs={{0,4},{1,3},{2,6},{3,1},{4,0},{5,7},{6,2},{7,5},{8,12},{9,11},{10,... | collective-permute-start | bytes 6291464 | tf_op jit(solution)/shard_map/ppermute | solution.py:125
  254.5 411.0 %reduce-scatter.7.cloned.1.call-start = ((), (), s32[]{:S(2)}) async-start(), calls=%async_computation.9 | async-start | bytes 2621440 | tf_op jit(solution)/shard_map/reduce_scatter | solution.py:163
  254.6 34.0 %collective-permute-start.33 = (bf16[512,2048]{1,0:T(8,128)(2,1)}, bf16[512,2048]{1,0:T(8,128)(2,1)S(1)}, u32[]{:S(2)}, u32[]{:S(2)}) collective-permute-start(bf16[512,2048]{1,0:T(8,128)(2,1)} %pad_maximum_fusion.2), channel_id=1, source_target_pairs={{0,1},{1,0},{2,3},{3,2},{4,5},{5,4},{6,7},{7,6},{8,9},{9,8},{10,11... | collective-permute-start | bytes 6291464 | tf_op jit(solution)/shard_map/ppermute | solution.py:125
  261.7 28.4 %collective-permute-start.34 = (bf16[512,2048]{1,0:T(8,128)(2,1)}, bf16[512,2048]{1,0:T(8,128)(2,1)S(1)}, u32[]{:S(2)}, u32[]{:S(2)}) collective-permute-start(bf16[512,2048]{1,0:T(8,128)(2,1)} %collective-permute-done.32), channel_id=1, source_target_pairs={{0,1},{1,0},{2,3},{3,2},{4,5},{5,4},{6,7},{7,6},{8,9},{9,8},{10,11... | collective-permute-start | bytes 6291464 | tf_op jit(solution)/shard_map/ppermute | solution.py:125
  261.8 35.3 %collective-permute-start.18 = (bf16[512,2048]{1,0:T(8,128)(2,1)}, bf16[512,2048]{1,0:T(8,128)(2,1)S(1)}, u32[]{:S(2)}, u32[]{:S(2)}) collective-permute-start(bf16[512,2048]{1,0:T(8,128)(2,1)} %pad_maximum_fusion.1), channel_id=1, source_target_pairs={{0,1},{1,0},{2,3},{3,2},{4,5},{5,4},{6,7},{7,6},{8,9},{9,8},{10,11... | collective-permute-start | bytes 6291464 | tf_op jit(solution)/shard_map/ppermute | solution.py:125
  276.4 22.1 %collective-permute-start.19 = (bf16[512,2048]{1,0:T(8,128)(2,1)}, bf16[512,2048]{1,0:T(8,128)(2,1)S(1)}, u32[]{:S(2)}, u32[]{:S(2)}) collective-permute-start(bf16[512,2048]{1,0:T(8,128)(2,1)} %collective-permute-done.17), channel_id=1, source_target_pairs={{0,1},{1,0},{2,3},{3,2},{4,5},{5,4},{6,7},{7,6},{8,9},{9,8},{10,11... | collective-permute-start | bytes 6291464 | tf_op jit(solution)/shard_map/ppermute | solution.py:125
  376.4 19.6 %collective-permute-start.36 = (bf16[512,2048]{1,0:T(8,128)(2,1)}, bf16[512,2048]{1,0:T(8,128)(2,1)}, u32[]{:S(2)}, u32[]{:S(2)}) collective-permute-start(bf16[512,2048]{1,0:T(8,128)(2,1)} %convolution_convert_fusion.1), channel_id=1, source_target_pairs={{0,1},{1,0},{2,3},{3,2},{4,5},{5,4},{6,7},{7,6},{8,9},{9,8},{10,11... | collective-permute-start | bytes 6291464 | tf_op jit(solution)/shard_map/ppermute | solution.py:125
  391.7 15.7 %collective-permute-start.27 = (bf16[512,2048]{1,0:T(8,128)(2,1)S(1)}, bf16[512,2048]{1,0:T(8,128)(2,1)S(1)}, u32[]{:S(2)}, u32[]{:S(2)}) collective-permute-start(bf16[512,2048]{1,0:T(8,128)(2,1)S(1)} %convolution_convert_fusion.3), channel_id=1, source_target_pairs={{0,1},{1,0},{2,3},{3,2},{4,5},{5,4},{6,7},{7,6},{8,9},{9,8},{10,11... | collective-permute-start | bytes 6291464 | tf_op jit(solution)/shard_map/ppermute | solution.py:125
  396.0 20.2 %collective-permute-start.35 = (bf16[512,2048]{1,0:T(8,128)(2,1)}, bf16[512,2048]{1,0:T(8,128)(2,1)S(1)}, u32[]{:S(2)}, u32[]{:S(2)}) collective-permute-start(bf16[512,2048]{1,0:T(8,128)(2,1)} %convolution_convert_fusion.2), channel_id=1, source_target_pairs={{0,1},{1,0},{2,3},{3,2},{4,5},{5,4},{6,7},{7,6},{8,9},{9,8},{10,11... | collective-permute-start | bytes 6291464 | tf_op jit(solution)/shard_map/ppermute | solution.py:125
  401.4 26.2 %collective-permute-start.37 = (bf16[512,2048]{1,0:T(8,128)(2,1)}, bf16[512,2048]{1,0:T(8,128)(2,1)S(1)}, u32[]{:S(2)}, u32[]{:S(2)}) collective-permute-start(bf16[512,2048]{1,0:T(8,128)(2,1)} %add_convert_fusion.2), channel_id=1, source_target_pairs={{0,4},{1,3},{2,6},{3,1},{4,0},{5,7},{6,2},{7,5},{8,12},{9,11},{10,... | collective-permute-start | bytes 6291464 | tf_op jit(solution)/shard_map/ppermute | solution.py:125
  407.1 25.9 %collective-permute-start.26 = (bf16[512,2048]{1,0:T(8,128)(2,1)}, bf16[512,2048]{1,0:T(8,128)(2,1)S(1)}, u32[]{:S(2)}, u32[]{:S(2)}) collective-permute-start(bf16[512,2048]{1,0:T(8,128)(2,1)} %convolution_convert_fusion.4), channel_id=1, source_target_pairs={{0,1},{1,0},{2,3},{3,2},{4,5},{5,4},{6,7},{7,6},{8,9},{9,8},{10,11... | collective-permute-start | bytes 6291464 | tf_op jit(solution)/shard_map/ppermute | solution.py:125
  411.0 50.4 %collective-permute-start.28 = (bf16[512,2048]{1,0:T(8,128)(2,1)}, bf16[512,2048]{1,0:T(8,128)(2,1)S(1)}, u32[]{:S(2)}, u32[]{:S(2)}) collective-permute-start(bf16[512,2048]{1,0:T(8,128)(2,1)} %add_convert_fusion.3), channel_id=1, source_target_pairs={{0,4},{1,3},{2,6},{3,1},{4,0},{5,7},{6,2},{7,5},{8,12},{9,11},{10,... | collective-permute-start | bytes 6291464 | tf_op jit(solution)/shard_map/ppermute | solution.py:125
  429.0 35.1 %collective-permute-start.38 = (bf16[256,2048]{1,0:T(8,128)(2,1)S(1)}, bf16[256,2048]{1,0:T(8,128)(2,1)S(1)}, u32[]{:S(2)}, u32[]{:S(2)}) collective-permute-start(bf16[256,2048]{1,0:T(8,128)(2,1)S(1)} %slice.470), channel_id=1, source_target_pairs={{0,2},{1,5},{2,0},{3,7},{4,6},{5,1},{6,4},{7,3},{8,10},{9,13},{10,... | collective-permute-start | bytes 3145736 | tf_op jit(solution)/shard_map/ppermute | solution.py:125
  462.5 14.9 %collective-permute-start.29 = (bf16[256,2048]{1,0:T(8,128)(2,1)S(1)}, bf16[256,2048]{1,0:T(8,128)(2,1)S(1)}, u32[]{:S(2)}, u32[]{:S(2)}) collective-permute-start(bf16[256,2048]{1,0:T(8,128)(2,1)S(1)} %slice.471), channel_id=1, source_target_pairs={{0,2},{1,5},{2,0},{3,7},{4,6},{5,1},{6,4},{7,3},{8,10},{9,13},{10,... | collective-permute-start | bytes 3145736 | tf_op jit(solution)/shard_map/ppermute | solution.py:125
  480.7 14.8 %collective-permute-start.39 = (bf16[256,2048]{1,0:T(8,128)(2,1)S(1)}, bf16[256,2048]{1,0:T(8,128)(2,1)S(1)}, u32[]{:S(2)}, u32[]{:S(2)}) collective-permute-start(bf16[256,2048]{1,0:T(8,128)(2,1)S(1)} %get-tuple-element.20), channel_id=1, source_target_pairs={{0,2},{1,5},{2,0},{3,7},{4,6},{5,1},{6,4},{7,3},{8,10},{9,13},{10,... | collective-permute-start | bytes 3145736 | tf_op jit(solution)/shard_map/ppermute | solution.py:125
  495.7 26.1 %collective-permute-start.40 = (bf16[512,2048]{1,0:T(8,128)(2,1)S(1)}, bf16[512,2048]{1,0:T(8,128)(2,1)S(1)}, u32[]{:S(2)}, u32[]{:S(2)}) collective-permute-start(bf16[512,2048]{1,0:T(8,128)(2,1)S(1)} %pad_maximum_fusion.3), channel_id=1, source_target_pairs={{0,4},{1,3},{2,6},{3,1},{4,0},{5,7},{6,2},{7,5},{8,12},{9,11},{10,... | collective-permute-start | bytes 6291464 | tf_op jit(solution)/shard_map/ppermute | solution.py:125
  497.3 27.4 %collective-permute-start.41 = (bf16[512,2048]{1,0:T(8,128)(2,1)S(1)}, bf16[512,2048]{1,0:T(8,128)(2,1)S(1)}, u32[]{:S(2)}, u32[]{:S(2)}) collective-permute-start(bf16[512,2048]{1,0:T(8,128)(2,1)S(1)} %pad_maximum_fusion.3), channel_id=1, source_target_pairs={{0,1},{1,0},{2,3},{3,2},{4,5},{5,4},{6,7},{7,6},{8,9},{9,8},{10,11... | collective-permute-start | bytes 6291464 | tf_op jit(solution)/shard_map/ppermute | solution.py:125
  535.1 188.5 %reduce-scatter.9.cloned.1.call-start = ((), (), s32[]{:S(2)}) async-start(), calls=%async_computation.10 | async-start | bytes 10485760 | tf_op jit(solution)/shard_map/reduce_scatter | solution.py:163
  549.8 321.4 %reduce-scatter.11.cloned.1.call-start = ((), (), s32[]{:S(2)}) async-start(), calls=%async_computation.11 | async-start | bytes 10485760 | tf_op jit(solution)/shard_map/reduce_scatter | solution.py:163
  564.6 420.3 %reduce-scatter.5.cloned.1.call-start = ((), (), s32[]{:S(2)}) async-start(), calls=%async_computation.8 | async-start | bytes 7864320 | tf_op jit(solution)/shard_map/reduce_scatter | solution.py:163
  630.1 26.4 %collective-permute-start.45 = (bf16[512,2048]{1,0:T(8,128)(2,1)}, bf16[512,2048]{1,0:T(8,128)(2,1)}, u32[]{:S(2)}, u32[]{:S(2)}) collective-permute-start(bf16[512,2048]{1,0:T(8,128)(2,1)} %add_convert_fusion.1), channel_id=1, source_target_pairs={{0,4},{1,3},{2,6},{3,1},{4,0},{5,7},{6,2},{7,5},{8,12},{9,11},{10,... | collective-permute-start | bytes 6291464 | tf_op jit(solution)/shard_map/ppermute | solution.py:125
  631.5 39.3 %collective-permute-start.30 = (bf16[256,2048]{1,0:T(8,128)(2,1)}, bf16[256,2048]{1,0:T(8,128)(2,1)}, u32[]{:S(2)}, u32[]{:S(2)}) collective-permute-start(bf16[256,2048]{1,0:T(8,128)(2,1)} %get-tuple-element.55), channel_id=1, source_target_pairs={{0,1},{1,0},{2,3},{3,2},{4,5},{5,4},{6,7},{7,6},{8,9},{9,8},{10,11... | collective-permute-start | bytes 3145736 | tf_op jit(solution)/shard_map/ppermute | solution.py:125
  662.5 26.2 %collective-permute-start.46 = (bf16[256,2048]{1,0:T(8,128)(2,1)}, bf16[256,2048]{1,0:T(8,128)(2,1)S(1)}, u32[]{:S(2)}, u32[]{:S(2)}) collective-permute-start(bf16[256,2048]{1,0:T(8,128)(2,1)} %slice.469), channel_id=1, source_target_pairs={{0,2},{1,5},{2,0},{3,7},{4,6},{5,1},{6,4},{7,3},{8,10},{9,13},{10,... | collective-permute-start | bytes 3145736 | tf_op jit(solution)/shard_map/ppermute | solution.py:125
  667.4 14.4 %collective-permute-start.52 = (f32[128,1,1,256]{3,0,2,1:T(8,128)}, f32[128,1,1,256]{3,0,2,1:T(8,128)}, u32[]{:S(2)}, u32[]{:S(2)}) collective-permute-start(f32[128,1,1,256]{3,0,2,1:T(8,128)} %get-tuple-element.85), channel_id=1, source_target_pairs={{0,2},{1,3},{2,0},{3,1},{4,6},{5,7},{6,4},{7,5},{8,10},{9,11},{10,... | collective-permute-start | bytes 393224 | tf_op jit(solution)/shard_map/ppermute | solution.py:125
  667.9 14.9 %collective-permute-start.53 = (f32[128,1,1,256]{3,0,2,1:T(8,128)}, f32[128,1,1,256]{3,0,2,1:T(8,128)}, u32[]{:S(2)}, u32[]{:S(2)}) collective-permute-start(f32[128,1,1,256]{3,0,2,1:T(8,128)} %get-tuple-element.84), channel_id=1, source_target_pairs={{0,4},{1,5},{2,6},{3,7},{4,0},{5,1},{6,2},{7,3},{8,12},{9,13},{10,... | collective-permute-start | bytes 393224 | tf_op jit(solution)/shard_map/ppermute | solution.py:125
  669.4 14.7 %collective-permute-start.54 = (f32[128,1,1,256]{3,0,2,1:T(8,128)}, f32[128,1,1,256]{3,0,2,1:T(8,128)}, u32[]{:S(2)}, u32[]{:S(2)}) collective-permute-start(f32[128,1,1,256]{3,0,2,1:T(8,128)} %get-tuple-element.83), channel_id=1, source_target_pairs={{0,6},{1,7},{2,4},{3,5},{4,2},{5,3},{6,0},{7,1},{8,14},{9,15},{10,... | collective-permute-start | bytes 393224 | tf_op jit(solution)/shard_map/ppermute | solution.py:125
  693.7 181.7 %collective-permute-start.48 = (f32[8,8192]{1,0:T(8,128)}, f32[8,8192]{1,0:T(8,128)}, u32[]{:S(2)}, u32[]{:S(2)}) collective-permute-start(f32[8,8192]{1,0:T(8,128)} %pad_maximum_fusion.5), channel_id=1, source_target_pairs={{0,1},{1,0},{2,3},{3,2},{4,5},{5,4},{6,7},{7,6},{8,9},{9,8},{10,11... | collective-permute-start | bytes 786440 | tf_op jit(solution)/shard_map/ppermute | solution.py:125
  726.6 150.3 %collective-permute-start.55 = (f32[128,1,1,1024]{3,0,2,1:T(8,128)}, f32[128,1,1,1024]{3,0,2,1:T(8,128)S(1)}, u32[]{:S(2)}, u32[]{:S(2)}) collective-permute-start(f32[128,1,1,1024]{3,0,2,1:T(8,128)} %get-tuple-element.52), channel_id=1, source_target_pairs={{0,2},{1,3},{2,0},{3,1},{4,6},{5,7},{6,4},{7,5},{8,10},{9,11},{10,... | collective-permute-start | bytes 1572872 | tf_op jit(solution)/shard_map/ppermute | solution.py:125
  728.1 149.4 %collective-permute-start.56 = (f32[128,1,1,1024]{3,0,2,1:T(8,128)}, f32[128,1,1,1024]{3,0,2,1:T(8,128)S(1)}, u32[]{:S(2)}, u32[]{:S(2)}) collective-permute-start(f32[128,1,1,1024]{3,0,2,1:T(8,128)} %get-tuple-element.51), channel_id=1, source_target_pairs={{0,4},{1,5},{2,6},{3,7},{4,0},{5,1},{6,2},{7,3},{8,12},{9,13},{10,... | collective-permute-start | bytes 1572872 | tf_op jit(solution)/shard_map/ppermute | solution.py:125
  734.4 263.1 %collective-permute-start.47 = (f32[256,2048]{1,0:T(8,128)}, f32[256,2048]{1,0:T(8,128)}, u32[]{:S(2)}, u32[]{:S(2)}) collective-permute-start(f32[256,2048]{1,0:T(8,128)} %get-tuple-element.18), channel_id=1, source_target_pairs={{0,1},{1,0},{2,3},{3,2},{4,5},{5,4},{6,7},{7,6},{8,9},{9,8},{10,11... | collective-permute-start | bytes 6291464 | tf_op jit(solution)/shard_map/ppermute | solution.py:125
  873.9 45.8 %collective-permute-start.58 = (f32[128,1,1,1024]{3,0,2,1:T(8,128)}, f32[128,1,1,1024]{3,0,2,1:T(8,128)}, u32[]{:S(2)}, u32[]{:S(2)}) collective-permute-start(f32[128,1,1,1024]{3,0,2,1:T(8,128)} %get-tuple-element.48), channel_id=1, source_target_pairs={{0,2},{1,3},{2,0},{3,1},{4,6},{5,7},{6,4},{7,5},{8,10},{9,11},{10,... | collective-permute-start | bytes 1572872 | tf_op jit(solution)/shard_map/ppermute | solution.py:125
  875.4 45.5 %collective-permute-start.59 = (f32[128,1,1,1024]{3,0,2,1:T(8,128)}, f32[128,1,1,1024]{3,0,2,1:T(8,128)}, u32[]{:S(2)}, u32[]{:S(2)}) collective-permute-start(f32[128,1,1,1024]{3,0,2,1:T(8,128)} %get-tuple-element.47), channel_id=1, source_target_pairs={{0,4},{1,5},{2,6},{3,7},{4,0},{5,1},{6,2},{7,3},{8,12},{9,13},{10,... | collective-permute-start | bytes 1572872 | tf_op jit(solution)/shard_map/ppermute | solution.py:125
  876.9 45.3 %collective-permute-start.60 = (f32[128,1,1,1024]{3,0,2,1:T(8,128)}, f32[128,1,1,1024]{3,0,2,1:T(8,128)}, u32[]{:S(2)}, u32[]{:S(2)}) collective-permute-start(f32[128,1,1,1024]{3,0,2,1:T(8,128)} %get-tuple-element.46), channel_id=1, source_target_pairs={{0,6},{1,7},{2,4},{3,5},{4,2},{5,3},{6,0},{7,1},{8,14},{9,15},{10,... | collective-permute-start | bytes 1572872 | tf_op jit(solution)/shard_map/ppermute | solution.py:125
  877.4 33.6 %collective-permute-start.57 = (f32[128,1,1,1024]{3,0,2,1:T(8,128)}, f32[128,1,1,1024]{3,0,2,1:T(8,128)}, u32[]{:S(2)}, u32[]{:S(2)}) collective-permute-start(f32[128,1,1,1024]{3,0,2,1:T(8,128)} %get-tuple-element.50), channel_id=1, source_target_pairs={{0,6},{1,7},{2,4},{3,5},{4,2},{5,3},{6,0},{7,1},{8,14},{9,15},{10,... | collective-permute-start | bytes 1572872 | tf_op jit(solution)/shard_map/ppermute | solution.py:125
  991.8 15.2 %collective-permute-start.49 = (f32[128,3,1,256]{3,0,2,1:T(8,128)}, f32[128,3,1,256]{3,0,2,1:T(8,128)}, u32[]{:S(2)}, u32[]{:S(2)}) collective-permute-start(f32[128,3,1,256]{3,0,2,1:T(8,128)} %bitcast.55), channel_id=1, source_target_pairs={{0,2},{1,3},{2,0},{3,1},{4,6},{5,7},{6,4},{7,5},{8,10},{9,11},{10,... | collective-permute-start | bytes 1179656 | tf_op jit(solution)/shard_map/ppermute | solution.py:125
  994.2 20.1 %collective-permute-start.50 = (f32[128,3,1,256]{3,0,2,1:T(8,128)}, f32[128,3,1,256]{3,0,2,1:T(8,128)}, u32[]{:S(2)}, u32[]{:S(2)}) collective-permute-start(f32[128,3,1,256]{3,0,2,1:T(8,128)} %bitcast.56), channel_id=1, source_target_pairs={{0,4},{1,5},{2,6},{3,7},{4,0},{5,1},{6,2},{7,3},{8,12},{9,13},{10,... | collective-permute-start | bytes 1179656 | tf_op jit(solution)/shard_map/ppermute | solution.py:125
  996.0 25.3 %collective-permute-start.51 = (f32[128,3,1,256]{3,0,2,1:T(8,128)S(1)}, f32[128,3,1,256]{3,0,2,1:T(8,128)S(1)}, u32[]{:S(2)}, u32[]{:S(2)}) collective-permute-start(f32[128,3,1,256]{3,0,2,1:T(8,128)S(1)} %bitcast.234), channel_id=1, source_target_pairs={{0,6},{1,7},{2,4},{3,5},{4,2},{5,3},{6,0},{7,1},{8,14},{9,15},{10,... | collective-permute-start | bytes 1179656 | tf_op jit(solution)/shard_map/ppermute | solution.py:125
  (84 other events, 1045.6 us)
Sparse Core Ops, SparseCore 0:
  40.5 63.8 all-gather.4
  106.5 26.6 all-gather.6
  159.6 78.4 all-gather.8
  254.6 85.6 all-gather.10
  535.2 42.2 reduce-scatter.6
  579.7 143.8 reduce-scatter.8
  725.9 145.2 reduce-scatter.10
  873.5 111.3 reduce-scatter.4
